TPU v7x, 32 devices: a whole 2x2x4 slice. The times are simulated.
32 devices in a mesh: groups: 2 (over x), tile: 16 (over z, y, core).
Axes of the slice: x: 2, y: 2, z: 4, core: 2. Of those that a mesh axis runs over, the one named last changes fastest.
Arguments:
- hidden: bfloat16 [12288, 1152], P(('groups', 'tile')), parts along dimension 0, may hold values from -40 to 40
- keep_mask: int32 [12288], P(('groups', 'tile')), parts along dimension 0, may hold values 0 or 1
- kept_embed: bfloat16 [1152], replicated, may hold values from -6 to 6
- time_mod: bfloat16 [50, 6, 1152], replicated, may hold values from -3 to 3
- timestep: int32 [2], P('groups'), parts along dimension 0, may hold values from 0 to 49
- qkv_weight: bfloat16 [1152, 3456], replicated, may hold values from -0.1875 to 0.1875
- proj_weight: bfloat16 [1152, 1152], replicated, may hold values from -0.1875 to 0.1875
- norm_gain: bfloat16 [1152], replicated, may hold values from 0.099609375 to 1.8984375
- in_weight: bfloat16 [1152, 5760], P('tile'), may hold values from -0.1875 to 0.1875
- in_bias: bfloat16 [5760], replicated, may hold values from -3 to 3
- conv_weight: bfloat16 [3, 3, 5760], replicated, may hold values from -2 to 2
- conv_bias: bfloat16 [5760], replicated, may hold values from -3 to 3
- out_weight: bfloat16 [2880, 1152], P(None, 'tile'), may hold values from -0.109375 to 0.109375
Outputs:
- output: bfloat16 [12288, 1152], P(('groups', 'tile')), parts along dimension 0
There are 2 independent parts, one for each index of `groups`. A program takes and returns all parts, laid end to end along the dimension named above; an argument that names none is the same for every part. Nothing has to cross between parts.
All inputs are finite; a program needn't handle non-finite values. No bound on the sum of `keep_mask` on one device may be relied on, other than what follows from the above.
Results may differ from a plain program's by a relative error of at most 0.0015.
The roundings to bfloat16 on the way count: a program that leaves them out, or rounds other values in their place, can miss the bound.
Values may be sent and summed in bfloat16 or wider, within the bound.
A program may use at most 192 MiB of HBM per device.

v0:
```python
import jax
import jax.numpy as jnp
from jax import lax
from jax.sharding import PartitionSpec as P

D = 1152
HEADS = 36
HEAD_DIM = 32
FF = 2880
CANVAS_W = 128


def padded_2(cells, sides, width):
    for axis, dim in sides:
        count = lax.axis_size(axis)
        ends = count - 1
        head = lax.slice_in_dim(cells, 0, width, axis=dim)
        tail = lax.slice_in_dim(cells, cells.shape[dim] - width, cells.shape[dim], axis=dim)
        cells = jnp.concatenate(
            [
                lax.ppermute(tail, axis, [(i, (i + 1) % count) for i in range(ends)]),
                cells,
                lax.ppermute(head, axis, [((i + 1) % count, i) for i in range(ends)]),
            ],
            axis=dim,
        )
    return cells


def modulated_norm(stream, shift, scale):
    factor = lax.rsqrt(jnp.mean(stream * stream, axis=-1, keepdims=True) + 1e-06)
    return stream * factor * (1.0 + scale) + shift


def convolve(window, conv_weight, conv_bias, count):
    width = window.shape[1] - 2
    total = jnp.zeros((count, width, window.shape[2]), jnp.float32) + conv_bias.astype(jnp.float32)
    for row_off in range(3):
        for col_off in range(3):
            total = total + window[row_off : row_off + count, col_off : col_off + width, :].astype(
                jnp.float32
            ) * conv_weight[row_off, col_off].astype(jnp.float32)
    return total


def row_folder(source, piece):
    return jnp.dot(source, piece, preferred_element_type=jnp.float32)


def local(
    hidden,
    keep_mask,
    kept_embed,
    time_mod,
    timestep,
    qkv_weight,
    proj_weight,
    norm_gain,
    in_weight,
    in_bias,
    conv_weight,
    conv_bias,
    out_weight,
):
    modulation = lax.dynamic_index_in_dim(time_mod, timestep[0], 0, keepdims=False).astype(
        jnp.float32
    )
    tokens = hidden.shape[0]
    rows = tokens // CANVAS_W
    stream = (
        hidden.astype(jnp.float32)
        + keep_mask.astype(jnp.float32)[:, None] * kept_embed.astype(jnp.float32)[None, :]
    )
    normed_in = modulated_norm(stream, modulation[0], modulation[1]).astype(jnp.bfloat16)
    mixed_qkv = jnp.dot(normed_in, qkv_weight, preferred_element_type=jnp.float32)
    query = jax.nn.relu(mixed_qkv[:, :D]).astype(jnp.bfloat16).reshape(tokens, HEADS, HEAD_DIM)
    key_rows = (
        jax.nn.relu(mixed_qkv[:, D : 2 * D]).astype(jnp.bfloat16).reshape(tokens, HEADS, HEAD_DIM)
    )
    values = mixed_qkv[:, 2 * D :].astype(jnp.bfloat16).reshape(tokens, HEADS, HEAD_DIM)
    local_state = jnp.einsum("thd,the->hde", key_rows, values, preferred_element_type=jnp.float32)
    state = lax.psum(local_state, "tile")
    attended = jnp.einsum(
        "thd,hde->the", query.astype(jnp.float32), state, precision=lax.Precision.HIGHEST
    ).reshape(tokens, D)
    factor = lax.rsqrt(jnp.mean(attended * attended, axis=-1, keepdims=True) + 1e-06)
    normed_attn = (attended * factor * norm_gain.astype(jnp.float32)).astype(jnp.bfloat16)
    after_attn = stream + modulation[2] * jnp.dot(
        normed_attn, proj_weight, preferred_element_type=jnp.float32
    )
    normed_ffn = modulated_norm(after_attn, modulation[3], modulation[4]).astype(jnp.bfloat16)
    before = row_folder(normed_ffn, lax.all_gather(in_weight, "tile", axis=0, tiled=True))
    inner = (
        jax.nn.silu(before + in_bias.astype(jnp.float32))
        .astype(jnp.bfloat16)
        .reshape(rows, CANVAS_W, 2 * FF)
    )
    framed = padded_2(inner, (("tile", 0),), 1)
    padded = jnp.pad(framed, ((0, 0), (1, 1), (0, 0)))
    conv = convolve(padded, conv_weight, conv_bias, rows)
    gated = (conv[..., :FF] * jax.nn.silu(conv[..., FF:])).astype(jnp.bfloat16).reshape(tokens, FF)
    projected = jnp.dot(
        gated,
        lax.all_gather(out_weight, "tile", axis=1, tiled=True),
        preferred_element_type=jnp.float32,
    )
    return (after_attn + modulation[5] * projected).astype(jnp.bfloat16)


def solution(mesh):
    in_specs = (
        P(("groups", "tile"), None),
        P(("groups", "tile")),
        P(),
        P(),
        P("groups"),
        P(),
        P(),
        P(),
        P("tile", None),
        P(),
        P(),
        P(),
        P(None, "tile"),
    )
    out_specs = P(("groups", "tile"), None)
    return jax.shard_map(local, mesh=mesh, in_specs=in_specs, out_specs=out_specs, check_vma=False)
```

profile of v0, /device:TPU:0, one launch (start us, length us, event | category | flops | bytes accessed | tf_op | source)
XLA Modules:
  0.0 325.5 jit_solution(18351720821955758159)
XLA Ops:
  7.3 0.9 dynamic-slice_convert_fusion
  10.3 1.6 multiply_reduce_fusion.1
  11.9 7.5 %fusion.15 = bf16[384,3456]{1,0:T(8,128)(2,1)S(1)} fusion(bf16[1152,3456]{1,0:T(8,128)(2,1)} %param.18, bf16[384,1152]{1,0:T(8,128)(2,1)} %param.13, f32[1152]{0:T(1024)S(1)} %get-tuple-element.17, f32[1152]{0:T(1024)S(1)} %get-tuple-element.18, f32[384]{0:T(512)S(1)} %add_rsqrt_fusion.2, f32[1152]{0:T(1024)S(1)} %convert_element_type.97, ...), kind=kOutput, calls=%fused_computation.36 | convolution fusion | flops 3060744192 | bytes 11518464 | tf_op jit(solution)/shard_map/dot_general | solution.py:75
  19.4 1.6 fusion.10
  21.0 1.7 copy.15
  22.8 2.2 copy.16
  25.0 2.4 fusion.26
  27.5 0.7 all-gather.3.cloned.1.call-update
  29.0 1.8 copy.17
  31.4 1.3 convert_element_type.106
  32.7 89.1 %all-reduce.3.cloned.1.call-done = f32[36,32,32]{1,2,0:T(8,128)} async-done(((f32[36,32,32]{1,2,0:T(8,128)}), f32[36,32,32]{1,2,0:T(8,128)}) %all-reduce.3.cloned.1.call-update) | async-done | bytes 147472 | tf_op jit(solution)/shard_map/psum | solution.py:82
  121.8 2.1 fusion.14
  124.2 2.9 multiply_reduce_fusion
  127.1 101.0 %all-gather.3.cloned.1.call-done = bf16[1152,5760]{1,0:T(8,128)(2,1)} async-done(((bf16[72,5760]{1,0:T(8,128)(2,1)}), bf16[1152,5760]{1,0:T(8,128)(2,1)}) %all-gather.3.cloned.1.call-update) | async-done | bytes 13271056 | tf_op jit(solution)/shard_map/all_gather | solution.py:92
  228.1 11.6 %multiply_convert_fusion = bf16[384,5760]{1,0:T(8,128)(2,1)S(1)} fusion(bf16[1152,5760]{1,0:T(8,128)(2,1)} %all-gather.3.cloned.1.call-done, f32[5760]{0:T(1024)S(1)} %copy-done.5, f32[384,1152]{1,0:T(8,128)} %get-tuple-element.28, f32[1152]{0:T(1024)S(1)} %copy-done.10, f32[1152]{0:T(1024)S(1)} %copy-done.11, f32[384]{0:T(512)S(1)} %add_rsqrt_fusion), kind=kOutput, calls=%fused_computation.7 | convolution fusion | flops 5111119872 | bytes 19497984 | tf_op jit(solution)/shard_map/dot_general | solution.py:47
  239.9 2.3 collective-permute-start
  242.2 1.5 collective-permute-start.1
  244.3 1.1 convert_reduce_fusion.8
  245.4 1.9 collective-permute-done.1
  247.4 3.0 fusion.5
  250.4 10.6 %multiply_add_fusion = f32[3,128,5760]{2,1,0:T(8,128)S(1)} fusion(bf16[3,128,5760]{2,1,0:T(8,128)(2,1)S(1)} %bitcast.35, bf16[5,130,5760]{2,1,0:T(8,128)(2,1)S(1)} %fusion.5, bf16[1,128,5760]{2,1,0:T(8,128)(2,1)} %copy-done.2, bf16[1,128,5760]{2,1,0:T(8,128)(2,1)S(1)} %collective-permute-done, f32[5760]{0:T(1024)} %get-tuple-element.12, ...), kind=kLoop, calls=%fused_computation.6 | loop fusion | flops 64143360 | bytes 42992640 | tf_op jit(solution)/shard_map/add | solution.py:40
  261.0 2.8 fusion.6
  263.8 46.9 %all-gather.5.cloned.1.call-done = bf16[2880,1152]{0,1:T(8,128)(2,1)} async-done(((bf16[2880,72]{0,1:T(8,128)(2,1)}), bf16[2880,1152]{0,1:T(8,128)(2,1)}) %all-gather.5.cloned.1.call-update) | async-done | bytes 6635536 | tf_op jit(solution)/shard_map/all_gather | solution.py:104
  310.7 8.4 %fusion.9 = bf16[384,1152]{1,0:T(8,128)(2,1)} fusion(f32[384,1152]{1,0:T(8,128)} %get-tuple-element.28, bf16[384,2880]{1,0:T(8,128)(2,1)} %bitcast.39, bf16[2880,1152]{0,1:T(8,128)(2,1)} %all-gather.5.cloned.1.call-done, f32[1152]{0:T(1024)S(1)} %copy-done.9), kind=kOutput, calls=%fused_computation.18 | convolution fusion | flops 2549366784 | bytes 11506176 | tf_op jit(solution)/shard_map/dot_general | solution.py:102
  (42 shorter events, 4.6 us)
Async XLA Ops:
  6.5 117.6 %copy-start = (bf16[1152,1152]{1,0:T(8,128)(2,1)S(1)}, bf16[1152,1152]{1,0:T(8,128)(2,1)}, u32[]{:S(2)}) copy-start(bf16[1152,1152]{1,0:T(8,128)(2,1)} %param.19) | copy-start | bytes 7962628
  6.5 115.3 %all-reduce.3.cloned.1.call-start = ((), (), s32[]{:S(2)}) async-start(), calls=%async_computation | async-start | bytes 1179648 | tf_op jit(solution)/shard_map/psum | solution.py:82
  10.3 9.1 %copy-start.7 = (f32[384]{0:T(512)}, f32[384]{0:T(512)S(1)}, u32[]{:S(2)}) copy-start(f32[384]{0:T(512)S(1)} %convert_element_type.96) | copy-start | bytes 4612
  27.5 200.6 %all-gather.3.cloned.1.call-start = ((), (), s32[]{:S(2)}) async-start(), calls=%async_computation.1 | async-start | bytes 14100480 | tf_op jit(solution)/shard_map/all_gather | solution.py:92
  28.2 282.4 %all-gather.5.cloned.1.call-start = ((), (), s32[]{:S(2)}) async-start(), calls=%async_computation.2 | async-start | bytes 7206912 | tf_op jit(solution)/shard_map/all_gather | solution.py:104
  121.8 2.4 copy-start.3
  121.8 2.4 copy-start.8
  121.8 2.4 copy-start.12
  124.1 103.9 %copy-start.5 = (f32[5760]{0:T(1024)S(1)}, f32[5760]{0:T(1024)}, u32[]{:S(2)}) copy-start(f32[5760]{0:T(1024)} %convert_element_type.106) | copy-start | bytes 69124
  124.2 103.9 %copy-start.10 = (f32[1152]{0:T(1024)S(1)}, f32[1152]{0:T(1024)}, u32[]{:S(2)}) copy-start(f32[1152]{0:T(1024)} %get-tuple-element.15) | copy-start | bytes 13828
  124.2 103.9 %copy-start.11 = (f32[1152]{0:T(1024)S(1)}, f32[1152]{0:T(1024)}, u32[]{:S(2)}) copy-start(f32[1152]{0:T(1024)} %get-tuple-element.16) | copy-start | bytes 13828
  239.7 4.0 %copy-start.6 = (bf16[5760]{0:T(1024)(128)(2,1)S(1)}, bf16[5760]{0:T(1024)(128)(2,1)}, u32[]{:S(2)}) copy-start(bf16[5760]{0:T(1024)(128)(2,1)} %param.24) | copy-start | bytes 34564
  239.7 4.6 %copy-start.4 = (bf16[3,3,5760]{2,1,0:T(4,128)(2,1)S(1)}, bf16[3,3,5760]{2,1,0:T(4,128)(2,1)}, u32[]{:S(2)}) copy-start(bf16[3,3,5760]{2,1,0:T(4,128)(2,1)} %param.23) | copy-start | bytes 311044
  239.9 5.5 %collective-permute-start = (bf16[1,128,5760]{2,1,0:T(8,128)(2,1)S(1)}, bf16[1,128,5760]{2,1,0:T(8,128)(2,1)S(1)}, u32[]{:S(2)}, u32[]{:S(2)}) collective-permute-start(bf16[1,128,5760]{2,1,0:T(8,128)(2,1)S(1)} %get-tuple-element.20), channel_id=1, source_target_pairs={{0,1},{1,2},{2,3},{3,4},{4,5},{5,6},{6,7},{7,8},{8,9},{9,10},{10,1... | collective-permute-start | bytes 4423688 | tf_op jit(solution)/shard_map/ppermute | solution.py:21
  242.2 5.2 %collective-permute-start.1 = (bf16[1,128,5760]{2,1,0:T(8,128)(2,1)S(1)}, bf16[1,128,5760]{2,1,0:T(8,128)(2,1)S(1)}, u32[]{:S(2)}, u32[]{:S(2)}) collective-permute-start(bf16[1,128,5760]{2,1,0:T(8,128)(2,1)S(1)} %get-tuple-element.21), channel_id=1, source_target_pairs={{1,0},{2,1},{3,2},{4,3},{5,4},{6,5},{7,6},{8,7},{9,8},{10,9},{11,1... | collective-permute-start | bytes 4423688 | tf_op jit(solution)/shard_map/ppermute | solution.py:23
  247.4 3.0 copy-start.2
  261.0 49.7 %copy-start.9 = (f32[1152]{0:T(1024)S(1)}, f32[1152]{0:T(1024)}, u32[]{:S(2)}) copy-start(f32[1152]{0:T(1024)} %get-tuple-element.14) | copy-start | bytes 13828
  310.7 8.4 %copy-start.1 = (bf16[1152,1152]{1,0:T(8,128)(2,1)S(1)}, bf16[1152,1152]{1,0:T(8,128)(2,1)}, u32[]{:S(2)}) copy-start(bf16[1152,1152]{1,0:T(8,128)(2,1)} %param.19) | copy-start | bytes 7962628
Sparse Core Ops, SparseCore 0:
  27.6 94.1 all-reduce.2
  124.0 104.0 all-gather.2
  230.2 80.3 all-gather.4
where the time goes:
time: 326 us
  waiting for transfers between devices  240 us (74%)
  matrix products  34.8 us (11%)
  other arithmetic  26.6 us (8%)
  between operations  14.1 us (4%)
  local copies, waits for them, and re-layouts  5.99 us (2%)
  starting transfers between devices  3.81 us (1%)
    all_gather x1, waiting for transfers between devices, local(): lax.all_gather(in_weight, 'tile', axis=0, tiled=True)  101 us
    psum x1, waiting for transfers between devices, local(): state = lax.psum(local_state, 'tile')  89.1 us
    all_gather x1, waiting for transfers between devices, local(): lax.all_gather(out_weight, 'tile', axis=1, tiled=True)  46.9 us
    dot_general x1, matrix products, row_folder(): return jnp.dot(source, piece, preferred_element_type=jnp.float32)  11.6 us
    add x1, other arithmetic, convolve(): total + window[row_off:row_off + count, col_off:col_off + width, :].astyp...  10.6 us
    dot_general x1, matrix products, local(): jnp.dot(gated, lax.all_gather(out_weight, 'tile', axis=1, tiled=True), pr...  8.36 us
    dot_general x1, matrix products, local(): jnp.dot(normed_in, qkv_weight, preferred_element_type=jnp.float32)  7.45 us
  transfers between devices with their start and end apart: 5, of which 4 were waited for; matrix products, arithmetic and copies ran while one was open for 12% of the time, Pallas kernels for 0%

commit v1 on v0

--- a/solution.py
+++ b/solution.py
@@ -79,7 +79,7 @@
     )
     values = mixed_qkv[:, 2 * D :].astype(jnp.bfloat16).reshape(tokens, HEADS, HEAD_DIM)
     local_state = jnp.einsum("thd,the->hde", key_rows, values, preferred_element_type=jnp.float32)
-    state = lax.psum(local_state, "tile")
+    state = jnp.sum(lax.all_gather(local_state, "tile"), axis=0)
     attended = jnp.einsum(
         "thd,hde->the", query.astype(jnp.float32), state, precision=lax.Precision.HIGHEST
     ).reshape(tokens, D)

time: 326 us -> 315 us (0.966)
  waiting for transfers between devices: 240 us -> 223 us
  other arithmetic: 26.6 us -> 32.3 us
    psum x1 -> x0, waiting for transfers between devices: 89.1 us -> none  [local(): state = lax.psum(local_state, 'tile')]
    all_gather x0 -> x1, waiting for transfers between devices: none -> 79.1 us  [local(): state = jnp.sum(lax.all_gather(local_state, 'tile'), axis=0)]
    all_gather x1, waiting for transfers between devices: 101 us -> 94.3 us  [local(): lax.all_gather(in_weight, 'tile', axis=0, tiled=True)]
    reduce_sum x0 -> x1, other arithmetic: none -> 5.74 us  [local(): state = jnp.sum(lax.all_gather(local_state, 'tile'), axis=0)]
  transfers between devices with their start and end apart: 5 -> 5, of which waited for: 4 -> 4; matrix products, arithmetic and copies ran while one was open for 12% -> 14% of each run, Pallas kernels for 0% -> 0%
where the time goes in v1:
time: 315 us
  waiting for transfers between devices  223 us (71%)
  matrix products  34.9 us (11%)
  other arithmetic  32.3 us (10%)
  between operations  14.1 us (4%)
  local copies, waits for them, and re-layouts  5.99 us (2%)
  starting transfers between devices  4.03 us (1%)
    all_gather x1, waiting for transfers between devices, local(): lax.all_gather(in_weight, 'tile', axis=0, tiled=True)  94.3 us
    all_gather x1, waiting for transfers between devices, local(): state = jnp.sum(lax.all_gather(local_state, 'tile'), axis=0)  79.1 us
    all_gather x1, waiting for transfers between devices, local(): lax.all_gather(out_weight, 'tile', axis=1, tiled=True)  46.9 us
    dot_general x1, matrix products, row_folder(): return jnp.dot(source, piece, preferred_element_type=jnp.float32)  11.6 us
    add x1, other arithmetic, convolve(): total + window[row_off:row_off + count, col_off:col_off + width, :].astyp...  10.6 us
    dot_general x1, matrix products, local(): jnp.dot(gated, lax.all_gather(out_weight, 'tile', axis=1, tiled=True), pr...  8.35 us
    dot_general x1, matrix products, local(): jnp.dot(normed_in, qkv_weight, preferred_element_type=jnp.float32)  7.45 us
  transfers between devices with their start and end apart: 5, of which 4 were waited for; matrix products, arithmetic and copies ran while one was open for 14% of the time, Pallas kernels for 0%

profile of v1, /device:TPU:0, one launch (start us, length us, event | category | flops | bytes accessed | tf_op | source)
XLA Modules:
  0.0 314.7 jit_solution(8181897770527916017)
XLA Ops:
  7.3 0.9 dynamic-slice_convert_fusion
  10.3 1.6 multiply_reduce_fusion.1
  11.9 7.4 %fusion.15 = bf16[384,3456]{1,0:T(8,128)(2,1)S(1)} fusion(bf16[1152,3456]{1,0:T(8,128)(2,1)} %param.18, bf16[384,1152]{1,0:T(8,128)(2,1)} %param.13, f32[1152]{0:T(1024)S(1)} %get-tuple-element.17, f32[1152]{0:T(1024)S(1)} %get-tuple-element.18, f32[384]{0:T(512)S(1)} %add_rsqrt_fusion.2, f32[1152]{0:T(1024)S(1)} %convert_element_type.97, ...), kind=kOutput, calls=%fused_computation.36 | convolution fusion | flops 3060744192 | bytes 11518464 | tf_op jit(solution)/shard_map/dot_general | solution.py:75
  19.4 1.6 fusion.10
  21.0 1.7 copy.20
  22.8 2.2 copy.21
  25.0 2.4 fusion.26
  29.0 1.8 copy.22
  31.4 1.3 convert_element_type.106
  32.7 79.1 %all-gather.9.cloned.1.call-done = f32[576,32,32]{2,1,0:T(8,128)} async-done(((f32[36,32,32]{2,1,0:T(8,128)}), f32[576,32,32]{2,1,0:T(8,128)}) %all-gather.9.cloned.1.call-update) | async-done | bytes 2359312 | tf_op jit(solution)/shard_map/all_gather | solution.py:82
  111.8 5.7 %reduce_sum.37 = f32[36,32,32]{2,1,0:T(8,128)} reduce(f32[16,36,32,32]{3,2,1,0:T(8,128)} %bitcast.37, f32[]{:T(128)} %constant.22.clone.1), dimensions={0}, to_apply=%region_1.2 | reduce | flops 552960 | bytes 2506756 | tf_op jit(solution)/shard_map/reduce_sum | solution.py:82
  117.5 2.1 fusion.14
  120.0 2.8 multiply_reduce_fusion
  122.9 94.3 %all-gather.5.cloned.1.call-done = bf16[1152,5760]{1,0:T(8,128)(2,1)} async-done(((bf16[72,5760]{1,0:T(8,128)(2,1)}), bf16[1152,5760]{1,0:T(8,128)(2,1)}) %all-gather.5.cloned.1.call-update) | async-done | bytes 13271056 | tf_op jit(solution)/shard_map/all_gather | solution.py:92
  217.2 11.6 %multiply_convert_fusion = bf16[384,5760]{1,0:T(8,128)(2,1)S(1)} fusion(bf16[1152,5760]{1,0:T(8,128)(2,1)} %all-gather.5.cloned.1.call-done, f32[5760]{0:T(1024)S(1)} %copy-done.5, f32[384,1152]{1,0:T(8,128)} %get-tuple-element.28, f32[1152]{0:T(1024)S(1)} %copy-done.10, f32[1152]{0:T(1024)S(1)} %copy-done.11, f32[384]{0:T(512)S(1)} %add_rsqrt_fusion), kind=kOutput, calls=%fused_computation.7 | convolution fusion | flops 5111119872 | bytes 19497984 | tf_op jit(solution)/shard_map/dot_general | solution.py:47
  229.1 2.3 collective-permute-start
  231.3 1.5 collective-permute-start.1
  233.5 1.1 convert_reduce_fusion.8
  234.6 1.9 collective-permute-done.1
  236.5 3.0 fusion.5
  239.5 10.6 %multiply_add_fusion = f32[3,128,5760]{2,1,0:T(8,128)S(1)} fusion(bf16[3,128,5760]{2,1,0:T(8,128)(2,1)S(1)} %bitcast.36, bf16[5,130,5760]{2,1,0:T(8,128)(2,1)S(1)} %fusion.5, bf16[1,128,5760]{2,1,0:T(8,128)(2,1)} %copy-done.2, bf16[1,128,5760]{2,1,0:T(8,128)(2,1)S(1)} %collective-permute-done, f32[5760]{0:T(1024)} %get-tuple-element.12, ...), kind=kLoop, calls=%fused_computation.6 | loop fusion | flops 64143360 | bytes 42992640 | tf_op jit(solution)/shard_map/add | solution.py:40
  250.1 2.8 fusion.6
  252.9 46.9 %all-gather.7.cloned.1.call-done = bf16[2880,1152]{0,1:T(8,128)(2,1)} async-done(((bf16[2880,72]{0,1:T(8,128)(2,1)}), bf16[2880,1152]{0,1:T(8,128)(2,1)}) %all-gather.7.cloned.1.call-update) | async-done | bytes 6635536 | tf_op jit(solution)/shard_map/all_gather | solution.py:104
  299.8 8.4 %fusion.9 = bf16[384,1152]{1,0:T(8,128)(2,1)} fusion(f32[384,1152]{1,0:T(8,128)} %get-tuple-element.28, bf16[384,2880]{1,0:T(8,128)(2,1)} %bitcast.41, bf16[2880,1152]{0,1:T(8,128)(2,1)} %all-gather.7.cloned.1.call-done, f32[1152]{0:T(1024)S(1)} %copy-done.9), kind=kOutput, calls=%fused_computation.18 | convolution fusion | flops 2549366784 | bytes 11506176 | tf_op jit(solution)/shard_map/dot_general | solution.py:102
  (43 shorter events, 5.3 us)
Async XLA Ops:
  6.5 113.4 %copy-start = (bf16[1152,1152]{1,0:T(8,128)(2,1)S(1)}, bf16[1152,1152]{1,0:T(8,128)(2,1)}, u32[]{:S(2)}) copy-start(bf16[1152,1152]{1,0:T(8,128)(2,1)} %param.19) | copy-start | bytes 7962628
  6.5 105.2 %all-gather.9.cloned.1.call-start = ((), (), s32[]{:S(2)}) async-start(), calls=%async_computation.2 | async-start | bytes 10027008 | tf_op jit(solution)/shard_map/all_gather | solution.py:82
  10.3 9.1 %copy-start.7 = (f32[384]{0:T(512)}, f32[384]{0:T(512)S(1)}, u32[]{:S(2)}) copy-start(f32[384]{0:T(512)S(1)} %convert_element_type.96) | copy-start | bytes 4612
  27.5 189.7 %all-gather.5.cloned.1.call-start = ((), (), s32[]{:S(2)}) async-start(), calls=%async_computation | async-start | bytes 14100480 | tf_op jit(solution)/shard_map/all_gather | solution.py:92
  28.2 271.5 %all-gather.7.cloned.1.call-start = ((), (), s32[]{:S(2)}) async-start(), calls=%async_computation.1 | async-start | bytes 7206912 | tf_op jit(solution)/shard_map/all_gather | solution.py:104
  117.5 2.5 copy-start.3
  117.5 2.5 copy-start.8
  117.5 2.5 copy-start.12
  119.9 97.2 %copy-start.5 = (f32[5760]{0:T(1024)S(1)}, f32[5760]{0:T(1024)}, u32[]{:S(2)}) copy-start(f32[5760]{0:T(1024)} %convert_element_type.106) | copy-start | bytes 69124
  119.9 97.2 %copy-start.10 = (f32[1152]{0:T(1024)S(1)}, f32[1152]{0:T(1024)}, u32[]{:S(2)}) copy-start(f32[1152]{0:T(1024)} %get-tuple-element.15) | copy-start | bytes 13828
  120.0 97.2 %copy-start.11 = (f32[1152]{0:T(1024)S(1)}, f32[1152]{0:T(1024)}, u32[]{:S(2)}) copy-start(f32[1152]{0:T(1024)} %get-tuple-element.16) | copy-start | bytes 13828
  228.8 4.0 %copy-start.6 = (bf16[5760]{0:T(1024)(128)(2,1)S(1)}, bf16[5760]{0:T(1024)(128)(2,1)}, u32[]{:S(2)}) copy-start(bf16[5760]{0:T(1024)(128)(2,1)} %param.24) | copy-start | bytes 34564
  228.8 4.6 %copy-start.4 = (bf16[3,3,5760]{2,1,0:T(4,128)(2,1)S(1)}, bf16[3,3,5760]{2,1,0:T(4,128)(2,1)}, u32[]{:S(2)}) copy-start(bf16[3,3,5760]{2,1,0:T(4,128)(2,1)} %param.23) | copy-start | bytes 311044
  229.1 5.5 %collective-permute-start = (bf16[1,128,5760]{2,1,0:T(8,128)(2,1)S(1)}, bf16[1,128,5760]{2,1,0:T(8,128)(2,1)S(1)}, u32[]{:S(2)}, u32[]{:S(2)}) collective-permute-start(bf16[1,128,5760]{2,1,0:T(8,128)(2,1)S(1)} %get-tuple-element.20), channel_id=1, source_target_pairs={{0,1},{1,2},{2,3},{3,4},{4,5},{5,6},{6,7},{7,8},{8,9},{9,10},{10,1... | collective-permute-start | bytes 4423688 | tf_op jit(solution)/shard_map/ppermute | solution.py:21
  231.3 5.2 %collective-permute-start.1 = (bf16[1,128,5760]{2,1,0:T(8,128)(2,1)S(1)}, bf16[1,128,5760]{2,1,0:T(8,128)(2,1)S(1)}, u32[]{:S(2)}, u32[]{:S(2)}) collective-permute-start(bf16[1,128,5760]{2,1,0:T(8,128)(2,1)S(1)} %get-tuple-element.21), channel_id=1, source_target_pairs={{1,0},{2,1},{3,2},{4,3},{5,4},{6,5},{7,6},{8,7},{9,8},{10,9},{11,1... | collective-permute-start | bytes 4423688 | tf_op jit(solution)/shard_map/ppermute | solution.py:23
  236.5 3.0 copy-start.2
  250.1 49.7 %copy-start.9 = (f32[1152]{0:T(1024)S(1)}, f32[1152]{0:T(1024)}, u32[]{:S(2)}) copy-start(f32[1152]{0:T(1024)} %get-tuple-element.14) | copy-start | bytes 13828
  299.8 8.4 %copy-start.1 = (bf16[1152,1152]{1,0:T(8,128)(2,1)S(1)}, bf16[1152,1152]{1,0:T(8,128)(2,1)}, u32[]{:S(2)}) copy-start(bf16[1152,1152]{1,0:T(8,128)(2,1)} %param.19) | copy-start | bytes 7962628
Sparse Core Ops, SparseCore 0:
  27.6 84.1 all-gather.8
  113.9 103.2 all-gather.4
  219.3 80.3 all-gather.6
